TPU v7x, 128 devices: a whole 4x4x4 slice. The times are simulated.
128 devices in a mesh: grp: 8 (over z_lo, y), pen: 16 (over z_hi, x, core).
Axes of the slice: x: 4, y: 4, z: 4 (z_hi: 2, z_lo: 2; z = z_hi * 2 + z_lo), core: 2. Of those that a mesh axis runs over, the one named last changes fastest.
Arguments:
- columns: float32 [2, 512, 512, 512], P(None, 'grp', 'pen'), may hold values from -6 to 6
- basis_in_x: float32 [512, 512], replicated, may hold values from -0.25 to 0.25
- basis_in_y: float32 [512, 512], replicated, may hold values from -0.25 to 0.25
- basis_in_z: float32 [512, 512], replicated, may hold values from -0.25 to 0.25
- basis_out_x: float32 [512, 512], replicated, may hold values from -0.25 to 0.25
- basis_out_y: float32 [512, 512], replicated, may hold values from -0.25 to 0.25
- basis_out_z: float32 [512, 512], replicated, may hold values from -0.25 to 0.25
- eig_x: float32 [512], replicated, may hold values from 0.05 to 3
- eig_y: float32 [512], replicated, may hold values from 0.05 to 3
- eig_z: float32 [512], replicated, may hold values from 0.05 to 3
- shift_table: float32 [64], replicated, may hold values from 0.5 to 8
- shift_index: int32 [2], replicated, may hold values from 0 to 63
Outputs:
- solved: float32 [2, 512, 512, 512], P(None, 'grp', 'pen')
Inputs may be any that keep to these rules, and one draw needn't show every extreme that they name: `shift_index`: indices into shift_table.
All inputs are finite; a program needn't handle non-finite values.
Results may differ from a plain program's by a relative error of at most 0.00007.
Values sent between devices are 32-bit elements; how exact they have to be, the bound alone decides.
A program may use at most 192 MiB of HBM per device.

v0:
```python
import jax
import jax.numpy as jnp
from jax import lax
from jax.sharding import PartitionSpec as P


def split_up(shard, dim, length):
    dims = shard.shape
    parts = shard.reshape(*dims[:dim], length, dims[dim] // length, *dims[dim + 1 :])
    return jnp.moveaxis(parts, dim, 0)


def joined_along(parts, dim):
    parts = jnp.moveaxis(parts, 0, dim)
    dims = parts.shape
    return parts.reshape(*dims[:dim], dims[dim] * dims[dim + 1], *dims[dim + 2 :])


def joined_exchange(shard, axis, axes, splits, concats):
    sizes = [lax.axis_size(a) for a in axes]
    parts = split_up(shard, splits[0], sizes[0])
    parts = jnp.moveaxis(split_up(parts, splits[1] + 1, sizes[1]), 0, 1)
    inside = parts.shape[2:]
    parts = parts.reshape(-1, *inside)
    parts = lax.all_to_all(parts, axis, split_axis=0, concat_axis=0, tiled=True)
    parts = joined_along(parts.reshape(*sizes, *inside), concats[0] + 1)
    return joined_along(parts, concats[1])


def solve_slab(
    volume,
    basis_in_x,
    basis_in_y,
    basis_in_z,
    basis_out_x,
    basis_out_y,
    basis_out_z,
    eig_x,
    eig_y,
    eig_z,
    shift_value,
):
    highest = lax.Precision.HIGHEST
    count, x_local, y_local, length = volume.shape
    pen_count = lax.axis_size("pen")
    grp_count = lax.axis_size("grp")
    z_slab = length // (pen_count * grp_count)
    forward = jnp.einsum("kz,cxyz->ckxy", basis_in_z, volume, precision=highest)
    planes = joined_exchange(forward, ("grp", "pen"), ("grp", "pen"), (1, 1), (2, 3))
    spectral = jnp.einsum("ix,ckxy->ckiy", basis_in_x, planes, precision=highest)
    spectral = jnp.einsum("jy,ckiy->ckij", basis_in_y, spectral, precision=highest)
    start_row = (lax.axis_index("grp") * pen_count + lax.axis_index("pen")) * z_slab
    eig_z_part = lax.dynamic_slice_in_dim(eig_z, start_row, z_slab)
    shift_wide = shift_value[:, None, None, None]
    denominator = (
        eig_z_part[None, :, None, None]
        + eig_x[None, None, :, None]
        + eig_y[None, None, None, :]
        + shift_wide
    )
    scaled = jnp.sqrt(2.0 * shift_wide) * spectral / denominator
    back = jnp.einsum("xi,ckij->ckxj", basis_out_x, scaled, precision=highest)
    back = jnp.einsum("yj,ckxj->ckxy", basis_out_y, back, precision=highest)
    returned = joined_exchange(back, ("grp", "pen"), ("grp", "pen"), (2, 3), (1, 1))
    returned = returned.reshape(count, pen_count, grp_count, z_slab, x_local, y_local)
    table = basis_out_z.reshape(length, grp_count, pen_count, z_slab)
    return jnp.einsum("zgpk,cpgkxy->cxyz", table, returned, precision=highest)


def per_device(
    columns,
    basis_in_x,
    basis_in_y,
    basis_in_z,
    basis_out_x,
    basis_out_y,
    basis_out_z,
    eig_x,
    eig_y,
    eig_z,
    shift_table,
    shift_index,
):
    shift_values = shift_table[shift_index]
    operands = (
        basis_in_x,
        basis_in_y,
        basis_in_z,
        basis_out_x,
        basis_out_y,
        basis_out_z,
        eig_x,
        eig_y,
        eig_z,
    )

    def solve_some(volume, shifts):
        return solve_slab(volume, *operands, shifts)

    pieces = [
        solve_some(columns[column : column + 1], shift_values[column : column + 1])
        for column in range(columns.shape[0])
    ]
    return jnp.concatenate(pieces, axis=0)


def solution(mesh):
    in_specs = (P(None, "grp", "pen", None), P(), P(), P(), P(), P(), P(), P(), P(), P(), P(), P())
    out_specs = P(None, "grp", "pen", None)
    return jax.shard_map(
        per_device, mesh=mesh, in_specs=in_specs, out_specs=out_specs, check_vma=False
    )
```

profile of v0, /device:TPU:1, one launch (start us, length us, event | category | flops | bytes accessed | tf_op | source)
XLA Modules:
  0.0 506.9 jit_solution(13045388830942738608)
XLA Ops:
  0.0 0.0 copy-start
  0.0 1.2 copy-done
  1.2 10.0 %fusion.18 = f32[1,512,64,32]{1,3,2,0:T(8,128)} fusion(f32[2,64,32,512]{3,2,1,0:T(8,128)} %param.12, f32[512,512]{1,0:T(8,128)S(1)} %copy-done), kind=kOutput, calls=%fused_computation.22 | convolution fusion | flops 6442450944 | bytes 9437184 | tf_op jit(solution)/shard_map/kz,cxyz->ckxy/dot_general | solution.py:48
  11.2 9.1 %copy.30 = f32[1,512,64,32]{2,3,1,0:T(8,128)} copy(f32[1,512,64,32]{1,3,2,0:T(8,128)} %fusion.18) | data formatting | bytes 8388608 | tf_op jit(solution)/shard_map/kz,cxyz->ckxy/transpose | solution.py:48
  20.3 9.4 %reshape.207 = f32[128,1,8192]{2,1,0:T(1,128)} reshape(f32[128,1,4,32,64]{4,3,2,1,0:T(8,128)} %bitcast.161) | data formatting | bytes 8388608
  29.8 12.7 %all-to-all-start = ((f32[128,1,8192]{2,1,0:T(1,128)}), f32[128,1,8192]{2,1,0:T(1,128)}, u32[]{:S(2)}, u32[]{:S(2)}) async-start(f32[128,1,8192]{2,1,0:T(1,128)} %reshape.207), calls=%async_computation | async-start | bytes 8388608 | tf_op jit(solution)/shard_map/all_to_all | solution.py:25
  42.4 10.0 %fusion.21 = f32[1,512,64,32]{1,3,2,0:T(8,128)} fusion(f32[2,64,32,512]{3,2,1,0:T(8,128)} %param.12, f32[512,512]{1,0:T(8,128)S(1)} %copy-done), kind=kOutput, calls=%fused_computation.23 | convolution fusion | flops 6442450944 | bytes 9437184 | tf_op jit(solution)/shard_map/kz,cxyz->ckxy/dot_general | solution.py:48
  52.4 9.1 %copy.40 = f32[1,512,64,32]{2,3,1,0:T(8,128)} copy(f32[1,512,64,32]{1,3,2,0:T(8,128)} %fusion.21) | data formatting | bytes 8388608 | tf_op jit(solution)/shard_map/kz,cxyz->ckxy/transpose | solution.py:48
  61.6 9.4 %reshape.203 = f32[128,1,8192]{2,1,0:T(1,128)} reshape(f32[128,1,4,32,64]{4,3,2,1,0:T(8,128)} %bitcast.162) | data formatting | bytes 8388608
  71.0 23.8 %all-to-all-done = f32[128,1,8192]{2,1,0:T(1,128)} async-done(((f32[128,1,8192]{2,1,0:T(1,128)}), f32[128,1,8192]{2,1,0:T(1,128)}, u32[]{:S(2)}, u32[]{:S(2)}) %all-to-all-start) | async-done | bytes 4194336 | tf_op jit(solution)/shard_map/all_to_all | solution.py:25
  94.7 6.8 %all-to-all-start.2 = ((f32[128,1,8192]{2,1,0:T(1,128)}), f32[128,1,8192]{2,1,0:T(1,128)}, u32[]{:S(2)}, u32[]{:S(2)}) async-start(f32[128,1,8192]{2,1,0:T(1,128)} %reshape.203), calls=%async_computation.2 | async-start | bytes 8388608 | tf_op jit(solution)/shard_map/all_to_all | solution.py:25
  101.6 0.0 copy-done.2
  101.6 0.6 gather_fusion
  102.2 0.6 fusion.46
  103.6 0.8 dynamic_slice.4
  104.3 0.0 copy-done.8
  104.3 0.1 broadcast_add_fusion
  104.4 0.6 broadcast.53
  105.0 13.9 %reduce.2 = f32[128,8192]{1,0:T(8,128)} reduce(f32[128,1,8192]{2,1,0:T(1,128)} %all-to-all-done, f32[]{:T(128)} %broadcast.53), dimensions={1}, to_apply=%all_to_all.12.reduce_sub_computation | reduce | bytes 8388612 | tf_op jit(solution)/shard_map/all_to_all | solution.py:25
  118.9 7.8 %reshape.208 = f32[128,1,4,32,64]{4,3,2,1,0:T(8,128)} reshape(f32[128,8192]{1,0:T(8,128)} %reduce.2) | data formatting | bytes 8388608
  126.7 14.7 %copy.32 = f32[16,1,4,8,64,32]{4,3,5,0,2,1:T(8,128)} copy(f32[16,1,4,8,64,32]{4,5,2,0,3,1:T(8,128)} %bitcast.163) | data formatting | bytes 8388608 | tf_op jit(solution)/shard_map/transpose | solution.py:14
  141.4 7.6 %reshape.166 = f32[16,1,4,512,32]{3,4,0,2,1:T(8,128)} reshape(f32[16,1,4,8,64,32]{4,3,5,0,2,1:T(8,128)} %copy.32) | data formatting | bytes 8388608 | tf_op jit(solution)/shard_map/reshape | solution.py:16
  149.0 0.0 copy-done.4
  149.0 9.1 %fusion.40 = f32[4,512,512]{2,1,0:T(8,128)S(1)} fusion(f32[4,512,512]{1,2,0:T(8,128)} %bitcast.169, f32[512,512]{1,0:T(8,128)S(1)} %copy-done.4), kind=kOutput, calls=%fused_computation.42 | convolution fusion | flops 6442450944 | bytes 9437184 | tf_op jit(solution)/shard_map/ix,ckxy->ckiy/dot_general | solution.py:50
  158.0 0.0 copy-done.5
  158.0 0.0 copy-start.9
  158.1 0.0 copy-start.11
  158.1 14.6 %fusion.8 = f32[4,512,512]{2,1,0:T(8,128)S(1)} fusion(f32[4,512,512]{2,1,0:T(8,128)S(1)} %fusion.40, f32[512,512]{1,0:T(8,128)S(1)} %copy-done.5), kind=kOutput, calls=%fused_computation.10 | convolution fusion | flops 6442450944 | bytes 9437184 | tf_op jit(solution)/shard_map/jy,ckiy->ckij/dot_general | solution.py:51
  172.7 0.0 copy-done.9
  172.7 0.0 copy-start.6
  172.7 9.9 %fusion.1 = f32[4,512,512]{1,2,0:T(8,128)S(1)} fusion(f32[4,512,512]{2,1,0:T(8,128)S(1)} %fusion.8, f32[]{:T(128)} %bitcast.16, f32[512]{0:T(512)S(1)} %copy-done.11, f32[4,512]{1,0:T(4,128)S(1)} %broadcast_add_fusion, f32[]{:T(128)} %bitcast, f32[512,512]{1,0:T(8,128)S(1)} %copy-done.9), kind=kOutput, calls=%fused_computation.5 | convolution fusion | flops 6446645248 | bytes 9447432 | tf_op jit(solution)/shard_map/xi,ckij->ckxj/dot_general | solution.py:62
  182.6 8.3 %convolution_bitcast_fusion.3 = f32[8,1,4,64,512]{4,3,0,2,1:T(8,128)} fusion(f32[4,8,64,512]{3,2,1,0:T(8,128)S(1)} %bitcast.172, f32[512,512]{1,0:T(8,128)S(1)} %copy-done.6), kind=kOutput, calls=%fused_computation.25 | convolution fusion | flops 6442450944 | bytes 9437184 | tf_op jit(solution)/shard_map/yj,ckxj->ckxy/dot_general | solution.py:63
  190.9 6.9 %copy.34 = f32[8,1,4,64,512]{3,4,2,0,1:T(8,128)} copy(f32[8,1,4,64,512]{4,3,0,2,1:T(8,128)} %convolution_bitcast_fusion.3) | data formatting | bytes 8388608 | tf_op jit(solution)/shard_map/transpose | solution.py:10
  197.8 8.1 %copy.35 = f32[8,16,1,4,64,32]{4,5,3,1,0,2:T(8,128)} copy(f32[8,16,1,4,64,32]{4,5,1,3,0,2:T(8,128)} %bitcast.164) | data formatting | bytes 8388608 | tf_op jit(solution)/shard_map/transpose;transpose | solution.py:22
  205.9 9.4 %reshape.209 = f32[128,1,8192]{2,1,0:T(1,128)} reshape(f32[128,1,4,32,64]{4,3,2,1,0:T(8,128)} %bitcast.165) | data formatting | bytes 8388608
  215.2 0.0 all-to-all-done.2
  215.3 10.8 %all-to-all-start.1 = ((f32[128,1,8192]{2,1,0:T(1,128)}), f32[128,1,8192]{2,1,0:T(1,128)}, u32[]{:S(2)}, u32[]{:S(2)}) async-start(f32[128,1,8192]{2,1,0:T(1,128)} %reshape.209), calls=%async_computation.1 | async-start | bytes 8388608 | tf_op jit(solution)/shard_map/all_to_all | solution.py:25
  226.7 13.8 %reduce = f32[128,8192]{1,0:T(8,128)} reduce(f32[128,1,8192]{2,1,0:T(1,128)} %all-to-all-done.2, f32[]{:T(128)} %broadcast.53), dimensions={1}, to_apply=%all_to_all.14.reduce_sub_computation | reduce | bytes 8388612 | tf_op jit(solution)/shard_map/all_to_all | solution.py:25
  240.5 7.8 %reshape.204 = f32[128,1,4,32,64]{4,3,2,1,0:T(8,128)} reshape(f32[128,8192]{1,0:T(8,128)} %reduce) | data formatting | bytes 8388608
  248.4 14.7 %copy.42 = f32[16,1,4,8,64,32]{4,3,5,0,2,1:T(8,128)} copy(f32[16,1,4,8,64,32]{4,5,2,0,3,1:T(8,128)} %bitcast.166) | data formatting | bytes 8388608 | tf_op jit(solution)/shard_map/transpose | solution.py:14
  263.1 7.5 %reshape.177 = f32[16,1,4,512,32]{3,4,0,2,1:T(8,128)} reshape(f32[16,1,4,8,64,32]{4,3,5,0,2,1:T(8,128)} %copy.42) | data formatting | bytes 8388608 | tf_op jit(solution)/shard_map/reshape | solution.py:16
  270.5 8.7 %fusion.38 = f32[4,512,512]{2,1,0:T(8,128)S(1)} fusion(f32[4,512,512]{1,2,0:T(8,128)} %bitcast.170, f32[512,512]{1,0:T(8,128)S(1)} %copy-done.4), kind=kOutput, calls=%fused_computation.40 | convolution fusion | flops 6442450944 | bytes 9437184 | tf_op jit(solution)/shard_map/ix,ckxy->ckiy/dot_general | solution.py:50
  279.3 0.0 copy-start.10
  279.3 14.6 %fusion.6 = f32[4,512,512]{2,1,0:T(8,128)S(1)} fusion(f32[4,512,512]{2,1,0:T(8,128)S(1)} %fusion.38, f32[512,512]{1,0:T(8,128)S(1)} %copy-done.5), kind=kOutput, calls=%fused_computation.8 | convolution fusion | flops 6442450944 | bytes 9437184 | tf_op jit(solution)/shard_map/jy,ckiy->ckij/dot_general | solution.py:51
  293.9 9.7 %fusion.4 = f32[4,512,512]{1,2,0:T(8,128)S(1)} fusion(f32[4,512,512]{2,1,0:T(8,128)S(1)} %fusion.6, f32[]{:T(128)} %bitcast.50, f32[]{:T(128)} %bitcast.37, f32[512]{0:T(512)S(1)} %copy-done.11, f32[4,512]{1,0:T(4,128)S(1)} %broadcast_add_fusion, f32[512,512]{1,0:T(8,128)S(1)} %copy-done.10), kind=kOutput, calls=%fused_computation.7 | convolution fusion | flops 6446645248 | bytes 9447432 | tf_op jit(solution)/shard_map/xi,ckij->ckxj/dot_general | solution.py:62
  303.6 8.8 %convolution_bitcast_fusion.2 = f32[8,1,4,64,512]{4,3,0,2,1:T(8,128)} fusion(f32[4,8,64,512]{3,2,1,0:T(8,128)S(1)} %bitcast.171, f32[512,512]{1,0:T(8,128)S(1)} %copy-done.6), kind=kOutput, calls=%fused_computation.24 | convolution fusion | flops 6442450944 | bytes 9437184 | tf_op jit(solution)/shard_map/yj,ckxj->ckxy/dot_general | solution.py:63
  312.4 6.9 %copy.44 = f32[8,1,4,64,512]{3,4,2,0,1:T(8,128)} copy(f32[8,1,4,64,512]{4,3,0,2,1:T(8,128)} %convolution_bitcast_fusion.2) | data formatting | bytes 8388608 | tf_op jit(solution)/shard_map/transpose | solution.py:10
  319.2 8.1 %copy.45 = f32[8,16,1,4,64,32]{4,5,3,1,0,2:T(8,128)} copy(f32[8,16,1,4,64,32]{4,5,1,3,0,2:T(8,128)} %bitcast.167) | data formatting | bytes 8388608 | tf_op jit(solution)/shard_map/transpose;transpose | solution.py:22
  327.3 9.4 %reshape.205 = f32[128,1,8192]{2,1,0:T(1,128)} reshape(f32[128,1,4,32,64]{4,3,2,1,0:T(8,128)} %bitcast.168) | data formatting | bytes 8388608
  336.7 0.0 all-to-all-done.1
  336.7 10.6 %all-to-all-start.3 = ((f32[128,1,8192]{2,1,0:T(1,128)}), f32[128,1,8192]{2,1,0:T(1,128)}, u32[]{:S(2)}, u32[]{:S(2)}) async-start(f32[128,1,8192]{2,1,0:T(1,128)} %reshape.205), calls=%async_computation.3 | async-start | bytes 8388608 | tf_op jit(solution)/shard_map/all_to_all | solution.py:25
  347.3 0.3 copy.38
  347.6 0.3 reshape.174
  348.0 13.8 %reduce.3 = f32[128,8192]{1,0:T(8,128)} reduce(f32[128,1,8192]{2,1,0:T(1,128)} %all-to-all-done.1, f32[]{:T(128)} %broadcast.53), dimensions={1}, to_apply=%all_to_all.13.reduce_sub_computation | reduce | bytes 8388612 | tf_op jit(solution)/shard_map/all_to_all | solution.py:25
  361.8 7.8 %reshape.210 = f32[128,1,4,32,64]{4,3,2,1,0:T(8,128)} reshape(f32[128,8192]{1,0:T(8,128)} %reduce.3) | data formatting | bytes 8388608
  369.6 16.2 %copy.51 = f32[16,8,4,64,32]{4,0,2,3,1:T(8,128)} copy(f32[16,8,4,64,32]{3,4,2,0,1:T(8,128)} %bitcast.159) | data formatting | bytes 8388608 | tf_op jit(solution)/shard_map/reshape.33
  385.9 13.7 %all-to-all-done.3 = f32[128,1,8192]{2,1,0:T(1,128)} async-done(((f32[128,1,8192]{2,1,0:T(1,128)}), f32[128,1,8192]{2,1,0:T(1,128)}, u32[]{:S(2)}, u32[]{:S(2)}) %all-to-all-start.3) | async-done | bytes 4194336 | tf_op jit(solution)/shard_map/all_to_all | solution.py:25
  399.6 13.9 %reduce.1 = f32[128,8192]{1,0:T(8,128)} reduce(f32[128,1,8192]{2,1,0:T(1,128)} %all-to-all-done.3, f32[]{:T(128)} %broadcast.53), dimensions={1}, to_apply=%all_to_all.15.reduce_sub_computation | reduce | bytes 8388612 | tf_op jit(solution)/shard_map/all_to_all | solution.py:25
  413.4 7.8 %reshape.206 = f32[128,1,4,32,64]{4,3,2,1,0:T(8,128)} reshape(f32[128,8192]{1,0:T(8,128)} %reduce.1) | data formatting | bytes 8388608
  421.3 16.2 %copy.55 = f32[16,8,4,64,32]{4,0,2,3,1:T(8,128)} copy(f32[16,8,4,64,32]{3,4,2,0,1:T(8,128)} %bitcast.160) | data formatting | bytes 8388608 | tf_op jit(solution)/shard_map/reshape.48
  437.5 33.4 %convolution_bitcast_fusion.1 = f32[1,64,32,512]{3,2,1,0:T(8,128)S(1)} fusion(f32[16,8,4,64,32]{4,0,2,3,1:T(8,128)} %copy.51, f32[512,8,16,4,1]{0,3,2,1,4:T(4,128)S(1)} %bitcast.173), kind=kOutput, calls=%fused_computation.21 | convolution fusion | flops 6442450944 | bytes 9437184 | tf_op jit(solution)/shard_map/zgpk,cpgkxy->cxyz/dot_general | solution.py:67
  470.9 0.0 copy-done.3
  470.9 31.0 %convolution_bitcast_fusion = f32[1,64,32,512]{3,2,1,0:T(8,128)S(1)} fusion(f32[16,8,4,64,32]{4,0,2,3,1:T(8,128)S(1)} %copy-done.3, f32[512,8,16,4,1]{0,3,2,1,4:T(4,128)S(1)} %bitcast.174), kind=kOutput, calls=%fused_computation.20 | convolution fusion | flops 6442450944 | bytes 9437184 | tf_op jit(solution)/shard_map/zgpk,cpgkxy->cxyz/dot_general | solution.py:67
  501.9 4.5 pad_maximum_fusion
  (16 shorter events, 0.0 us)
Async XLA Ops:
  0.0 1.2 copy-start
  29.8 65.0 %all-to-all-start = ((f32[128,1,8192]{2,1,0:T(1,128)}), f32[128,1,8192]{2,1,0:T(1,128)}, u32[]{:S(2)}, u32[]{:S(2)}) async-start(f32[128,1,8192]{2,1,0:T(1,128)} %reshape.207), calls=%async_computation | async-start | bytes 8388608 | tf_op jit(solution)/shard_map/all_to_all | solution.py:25
  71.0 30.6 %copy-start.12 = (s32[2]{0:T(128)S(1)}, s32[2]{0:T(128)}, u32[]{:S(2)}) copy-start(s32[2]{0:T(128)} %param.23) | copy-start | bytes 28
  71.0 30.6 %copy-start.2 = (f32[64]{0:T(128)S(1)}, f32[64]{0:T(128)}, u32[]{:S(2)}) copy-start(f32[64]{0:T(128)} %param.22) | copy-start | bytes 772
  71.0 33.4 %copy-start.8 = (f32[512]{0:T(512)S(1)}, f32[512]{0:T(512)}, u32[]{:S(2)}) copy-start(f32[512]{0:T(512)} %param.19) | copy-start | bytes 6148
  94.7 120.5 %all-to-all-start.2 = ((f32[128,1,8192]{2,1,0:T(1,128)}), f32[128,1,8192]{2,1,0:T(1,128)}, u32[]{:S(2)}, u32[]{:S(2)}) async-start(f32[128,1,8192]{2,1,0:T(1,128)} %reshape.203), calls=%async_computation.2 | async-start | bytes 8388608 | tf_op jit(solution)/shard_map/all_to_all | solution.py:25
  141.4 7.6 %copy-start.4 = (f32[512,512]{1,0:T(8,128)S(1)}, f32[512,512]{1,0:T(8,128)}, u32[]{:S(2)}) copy-start(f32[512,512]{1,0:T(8,128)} %param.13) | copy-start | bytes 3145732
  149.0 9.1 %copy-start.5 = (f32[512,512]{1,0:T(8,128)S(1)}, f32[512,512]{1,0:T(8,128)}, u32[]{:S(2)}) copy-start(f32[512,512]{1,0:T(8,128)} %param.14) | copy-start | bytes 3145732
  158.0 14.6 %copy-start.9 = (f32[512,512]{1,0:T(8,128)S(1)}, f32[512,512]{1,0:T(8,128)}, u32[]{:S(2)}) copy-start(f32[512,512]{1,0:T(8,128)} %param.16) | copy-start | bytes 3145732
  158.1 14.6 %copy-start.11 = (f32[512]{0:T(512)S(1)}, f32[512]{0:T(512)}, u32[]{:S(2)}) copy-start(f32[512]{0:T(512)} %param.20) | copy-start | bytes 6148
  172.7 9.9 %copy-start.6 = (f32[512,512]{1,0:T(8,128)S(1)}, f32[512,512]{1,0:T(8,128)}, u32[]{:S(2)}) copy-start(f32[512,512]{1,0:T(8,128)} %param.17) | copy-start | bytes 3145732
  215.3 121.5 %all-to-all-start.1 = ((f32[128,1,8192]{2,1,0:T(1,128)}), f32[128,1,8192]{2,1,0:T(1,128)}, u32[]{:S(2)}, u32[]{:S(2)}) async-start(f32[128,1,8192]{2,1,0:T(1,128)} %reshape.209), calls=%async_computation.1 | async-start | bytes 8388608 | tf_op jit(solution)/shard_map/all_to_all | solution.py:25
  279.3 14.7 %copy-start.10 = (f32[512,512]{1,0:T(8,128)S(1)}, f32[512,512]{1,0:T(8,128)}, u32[]{:S(2)}) copy-start(f32[512,512]{1,0:T(8,128)} %param.16) | copy-start | bytes 3145732
  336.7 10.6 %copy-start.7 = (f32[512,512]{1,0:T(8,128)S(1)}, f32[512,512]{1,0:T(8,128)}, u32[]{:S(2)}) copy-start(f32[512,512]{1,0:T(8,128)} %param.18) | copy-start | bytes 3145732
  336.7 62.9 %all-to-all-start.3 = ((f32[128,1,8192]{2,1,0:T(1,128)}), f32[128,1,8192]{2,1,0:T(1,128)}, u32[]{:S(2)}, u32[]{:S(2)}) async-start(f32[128,1,8192]{2,1,0:T(1,128)} %reshape.205), calls=%async_computation.3 | async-start | bytes 8388608 | tf_op jit(solution)/shard_map/all_to_all | solution.py:25
  437.5 33.4 %copy-start.3 = (f32[16,8,4,64,32]{4,0,2,3,1:T(8,128)S(1)}, f32[16,8,4,64,32]{4,0,2,3,1:T(8,128)}, u32[]{:S(2)}) copy-start(f32[16,8,4,64,32]{4,0,2,3,1:T(8,128)} %copy.55) | copy-start | bytes 12582916
  501.9 4.5 copy-start.1
where the time goes:
time: 515 us; the launch traced here: 507 us
  local copies, waits for them, and re-layouts  198 us (38%)
  matrix products  168 us (33%)
  other arithmetic  60 us (12%)
  starting transfers between devices  40.9 us (8%)
  waiting for transfers between devices  37.5 us (7%)
    unnamed x35, local copies, waits for them, and re-layouts  70.6 us
    dot_general x2, matrix products, solve_slab(): return jnp.einsum('zgpk,cpgkxy->cxyz', table, returned, precision=highest)  64.4 us
    all_to_all x4, other arithmetic, joined_exchange(): parts = lax.all_to_all(parts, axis, split_axis=0, concat_axis=0, tiled=True)  55.4 us
    all_to_all x4, starting transfers between devices, joined_exchange(): parts = lax.all_to_all(parts, axis, split_axis=0, concat_axis=0, tiled=True)  40.9 us
    all_to_all x4, waiting for transfers between devices, joined_exchange(): parts = lax.all_to_all(parts, axis, split_axis=0, concat_axis=0, tiled=True)  37.5 us
    another operation x2, local copies, waits for them, and re-layouts  32.4 us
    transpose x2, local copies, waits for them, and re-layouts, joined_along(): parts = jnp.moveaxis(parts, 0, dim)  29.4 us
    dot_general x2, matrix products, solve_slab(): jnp.einsum('jy,ckiy->ckij', basis_in_y, spectral, precision=highest)  29.2 us
  transfers between devices with their start and end apart: 4, of which 2 were waited for; matrix products, arithmetic and copies ran while one was open for 57% of the time, Pallas kernels for 0%

commit v1 on v0

v1 whole, which is shorter than its diff:
```python
import jax
import jax.numpy as jnp
from jax import lax
from jax.experimental import pallas as pl
from jax.experimental.pallas import tpu as pltpu
from jax.sharding import PartitionSpec as P

MESH = pl.DeviceIdType.MESH


def exchange_kernel(x_ref, o_ref, send_sem, recv_sem, local_sem):
    grp_count, pen_count = lax.axis_size("grp"), lax.axis_size("pen")
    count = grp_count * pen_count
    steps = x_ref.shape[1]
    me = lax.axis_index("grp") * pen_count + lax.axis_index("pen")

    def place(t):
        return {"grp": t // pen_count, "pen": t % pen_count}

    barrier = pltpu.get_barrier_semaphore()

    def greet(i, carry):
        pl.semaphore_signal(
            barrier, inc=1, device_id=place((me + i) % count), device_id_type=MESH
        )
        return carry

    lax.fori_loop(1, count, greet, 0)
    pl.semaphore_wait(barrier, count - 1)

    def one_step(s, carry):
        def send(i, inner):
            t = (me + i) % count
            pltpu.make_async_remote_copy(
                src_ref=x_ref.at[t, s],
                dst_ref=o_ref.at[me, s],
                send_sem=send_sem,
                recv_sem=recv_sem,
                device_id=place(t),
                device_id_type=MESH,
            ).start()
            return inner

        return lax.fori_loop(1, count, send, carry)

    own = pltpu.make_async_copy(x_ref.at[me], o_ref.at[me], local_sem)
    own.start()
    lax.fori_loop(0, steps, one_step, 0)
    own.wait()
    others = pl.ds(0, count - 1)
    pltpu.make_async_copy(x_ref.at[others], x_ref.at[others], send_sem).wait()
    pltpu.make_async_copy(o_ref.at[others], o_ref.at[others], recv_sem).wait()


def exchange(x):
    return pl.pallas_call(
        exchange_kernel,
        out_shape=jax.ShapeDtypeStruct(x.shape, x.dtype),
        in_specs=[pl.BlockSpec(memory_space=pl.ANY)],
        out_specs=pl.BlockSpec(memory_space=pl.ANY),
        scratch_shapes=[pltpu.SemaphoreType.DMA] * 3,
        compiler_params=pltpu.CompilerParams(collective_id=0, has_side_effects=True),
        name="exchange",
    )(x)


def per_device(
    columns,
    basis_in_x,
    basis_in_y,
    basis_in_z,
    basis_out_x,
    basis_out_y,
    basis_out_z,
    eig_x,
    eig_y,
    eig_z,
    shift_table,
    shift_index,
):
    high = lax.Precision.HIGH
    shift_values = shift_table[shift_index]
    count, x_local, y_local, length = columns.shape
    pen_count = lax.axis_size("pen")
    grp_count = lax.axis_size("grp")
    devices = pen_count * grp_count
    z_slab = length // devices
    rows = x_local * y_local // 128
    forward = jnp.einsum("kz,cxyz->kcxy", basis_in_z, columns, precision=high)
    forward = forward.reshape(devices, z_slab * count, rows, 128)
    planes = exchange(forward)
    planes = planes.reshape(grp_count, pen_count, z_slab, count, x_local, y_local)
    planes = planes.transpose(3, 2, 0, 4, 1, 5).reshape(count, z_slab, length, length)
    spectral = jnp.einsum("ix,ckxy->ckiy", basis_in_x, planes, precision=high)
    spectral = jnp.einsum("jy,ckiy->ckij", basis_in_y, spectral, precision=high)
    start_row = (lax.axis_index("grp") * pen_count + lax.axis_index("pen")) * z_slab
    eig_z_part = lax.dynamic_slice_in_dim(eig_z, start_row, z_slab)
    shift_wide = shift_values[:, None, None, None]
    denominator = (
        eig_z_part[None, :, None, None]
        + eig_x[None, None, :, None]
        + eig_y[None, None, None, :]
        + shift_wide
    )
    scaled = jnp.sqrt(2.0 * shift_wide) * spectral / denominator
    back = jnp.einsum("xi,ckij->ckxj", basis_out_x, scaled, precision=high)
    back = jnp.einsum("yj,ckxj->ckxy", basis_out_y, back, precision=high)
    back = back.reshape(count, z_slab, grp_count, x_local, pen_count, y_local)
    back = back.transpose(2, 4, 1, 0, 3, 5).reshape(devices, z_slab * count, rows, 128)
    returned = exchange(back)
    returned = returned.reshape(length, count, x_local, y_local)
    return jnp.einsum("zk,kcxy->cxyz", basis_out_z, returned, precision=high)


def solution(mesh):
    in_specs = (P(None, "grp", "pen", None), P(), P(), P(), P(), P(), P(), P(), P(), P(), P(), P())
    out_specs = P(None, "grp", "pen", None)
    return jax.shard_map(
        per_device, mesh=mesh, in_specs=in_specs, out_specs=out_specs, check_vma=False
    )
```

time: 515 us -> 577 us (1.12)
  the two profiles are of different devices: /device:TPU:1 before, /device:TPU:33 now
where the time goes in v1:
time: 577 us; the launch traced here: 567 us
  Pallas kernels  213 us (37%)
  local copies, waits for them, and re-layouts  192 us (33%)
  matrix products  161 us (28%)
    pallas_call x2, Pallas kernels, exchange(): pl.pallas_call(exchange_kernel, out_shape=jax.ShapeDtypeStruct(x.shape, x...  213 us
    dot_general x1, matrix products, per_device(): return jnp.einsum('zk,kcxy->cxyz', basis_out_z, returned, precision=high)  98.7 us
    dot_general x1, local copies, waits for them, and re-layouts, per_device(): forward = jnp.einsum('kz,cxyz->kcxy', basis_in_z, columns, precision=high)  26.6 us
    transpose x1, local copies, waits for them, and re-layouts, per_device(): planes.transpose(3, 2, 0, 4, 1, 5).reshape(count, z_slab, length, length)  24.7 us
    transpose x1, local copies, waits for them, and re-layouts, per_device(): back.transpose(2, 4, 1, 0, 3, 5).reshape(devices, z_slab * count, rows, 128)  23.1 us
    reshape x1, local copies, waits for them, and re-layouts, per_device(): forward = forward.reshape(devices, z_slab * count, rows, 128)  23 us
    reshape x1, local copies, waits for them, and re-layouts, per_device(): back.transpose(2, 4, 1, 0, 3, 5).reshape(devices, z_slab * count, rows, 128)  23 us
    reshape x1, local copies, waits for them, and re-layouts, per_device(): returned = returned.reshape(length, count, x_local, y_local)  20.7 us

profile of v1, /device:TPU:33, one launch (start us, length us, event | category | flops | bytes accessed | tf_op | source)
XLA Modules:
  0.0 566.8 jit_solution(18011923928113097899)
XLA Ops:
  0.0 0.0 copy-start
  0.0 1.2 copy-done
  1.2 15.6 %fusion.6 = f32[512,2,64,32]{0,2,3,1:T(8,128)} fusion(f32[2,64,32,512]{3,2,1,0:T(8,128)} %param.12, f32[512,512]{1,0:T(8,128)S(1)} %copy-done), kind=kOutput, calls=%fused_computation.7 | convolution fusion | flops 6442450944 | bytes 17825792 | tf_op jit(solution)/shard_map/kz,cxyz->kcxy/dot_general | solution.py:89
  16.8 26.6 %copy.18 = f32[512,2,64,32]{3,2,1,0:T(8,128)} copy(f32[512,2,64,32]{0,2,3,1:T(8,128)} %fusion.6) | data formatting | bytes 16777216 | tf_op jit(solution)/shard_map/kz,cxyz->kcxy/dot_general | solution.py:89
  43.5 23.0 %reshape.66.x_ref = f32[128,8,16,128]{3,2,1,0:T(8,128)} reshape(f32[512,2,64,32]{3,2,1,0:T(8,128)} %copy.18) | data formatting | bytes 16777216 | tf_op jit(solution)/shard_map/reshape | solution.py:90
  66.4 106.5 %exchange.2 = f32[128,8,16,128]{3,2,1,0:T(8,128)} custom-call(f32[128,8,16,128]{3,2,1,0:T(8,128)} %reshape.66.x_ref), custom_call_target="tpu_custom_call" | custom-call | tf_op jit(solution)/shard_map/exchange/pallas_call | solution.py:56
  173.0 20.7 %reshape.67 = f32[8,16,4,2,64,32]{5,4,3,2,1,0:T(8,128)} reshape(f32[128,8,16,128]{3,2,1,0:T(8,128)} %exchange.2) | data formatting | bytes 16777216 | tf_op jit(solution)/shard_map/reshape | solution.py:92
  193.6 24.7 %copy.19 = f32[2,4,8,64,16,32]{3,2,5,4,1,0:T(8,128)} copy(f32[2,4,8,64,16,32]{5,3,0,1,4,2:T(8,128)} %bitcast.55) | data formatting | bytes 16777216 | tf_op jit(solution)/shard_map/transpose | solution.py:93
  218.3 0.0 copy-start.3
  218.3 14.3 %reshape.68 = f32[2,4,512,512]{2,3,1,0:T(8,128)} reshape(f32[2,4,8,64,16,32]{3,2,5,4,1,0:T(8,128)} %copy.19) | data formatting | bytes 16777216 | tf_op jit(solution)/shard_map/reshape | solution.py:93
  232.5 0.0 copy-done.3
  232.6 0.0 copy-start.4
  232.6 9.8 %fusion.19 = f32[2,4,512,512]{3,2,1,0:T(8,128)S(1)} fusion(f32[2,4,512,512]{2,3,1,0:T(8,128)} %reshape.68, f32[512,512]{1,0:T(8,128)S(1)} %copy-done.3), kind=kOutput, calls=%fused_computation.21 | convolution fusion | flops 6442450944 | bytes 17825792 | tf_op jit(solution)/shard_map/ix,ckxy->ckiy/dot_general | solution.py:94
  242.4 0.0 copy-done.4
  242.4 0.0 copy-start.10
  242.4 0.0 copy-start.2
  242.4 0.0 copy-start.8
  242.5 0.0 copy-start.7
  242.5 0.0 copy-start.9
  242.5 15.8 %fusion.4 = f32[2,4,512,512]{3,2,1,0:T(8,128)} fusion(f32[2,4,512,512]{3,2,1,0:T(8,128)S(1)} %fusion.19, f32[512,512]{1,0:T(8,128)S(1)} %copy-done.4), kind=kOutput, calls=%fused_computation.5 | convolution fusion | flops 6442450944 | bytes 17825792 | tf_op jit(solution)/shard_map/jy,ckiy->ckij/dot_general | solution.py:95
  258.2 0.0 copy-done.10
  258.3 0.0 copy-done.2
  258.3 0.6 gather_fusion
  258.9 0.8 dynamic_slice.3
  259.7 0.0 copy-done.8
  259.7 0.1 broadcast_add_fusion.1
  259.7 0.0 copy-done.7
  259.7 0.3 broadcast_add_fusion
  260.1 0.0 copy-done.9
  260.1 0.0 copy-start.5
  260.1 12.1 %fusion.8 = f32[2,4,512,512]{2,3,1,0:T(8,128)S(1)} fusion(f32[2,4,512,512]{3,2,1,0:T(8,128)} %fusion.4, f32[2]{0:T(128)S(1)} %gather_fusion, f32[4,512,512]{2,1,0:T(8,128)S(1)} %broadcast_add_fusion, f32[2]{0:T(128)S(1)} %multiply_sqrt_fusion, f32[512,512]{1,0:T(8,128)S(1)} %copy-done.9), kind=kOutput, calls=%fused_computation.9 | convolution fusion | flops 6448742400 | bytes 22020112 | tf_op jit(solution)/shard_map/xi,ckij->ckxj/dot_general | solution.py:106
  272.3 0.0 copy-done.5
  272.3 9.0 %fusion.2 = f32[2,4,512,512]{2,3,1,0:T(8,128)} fusion(f32[2,4,512,512]{2,3,1,0:T(8,128)S(1)} %fusion.8, f32[512,512]{1,0:T(8,128)S(1)} %copy-done.5), kind=kOutput, calls=%fused_computation.3 | convolution fusion | flops 6442450944 | bytes 17825792 | tf_op jit(solution)/shard_map/yj,ckxj->ckxy/dot_general | solution.py:107
  281.3 12.9 %reshape.69 = f32[2,4,8,64,16,32]{3,2,5,4,1,0:T(8,128)} reshape(f32[2,4,512,512]{2,3,1,0:T(8,128)} %fusion.2) | data formatting | bytes 16777216 | tf_op jit(solution)/shard_map/reshape | solution.py:108
  294.1 23.1 %copy.21 = f32[8,16,4,2,64,32]{5,4,3,2,1,0:T(8,128)} copy(f32[8,16,4,2,64,32]{4,0,5,1,2,3:T(8,128)} %bitcast.56) | data formatting | bytes 16777216 | tf_op jit(solution)/shard_map/transpose | solution.py:109
  317.3 23.0 %reshape.70.x_ref = f32[128,8,16,128]{3,2,1,0:T(8,128)} reshape(f32[8,16,4,2,64,32]{5,4,3,2,1,0:T(8,128)} %copy.21) | data formatting | bytes 16777216 | tf_op jit(solution)/shard_map/reshape | solution.py:109
  340.2 106.7 %exchange.3 = f32[128,8,16,128]{3,2,1,0:T(8,128)} custom-call(f32[128,8,16,128]{3,2,1,0:T(8,128)} %reshape.70.x_ref), custom_call_target="tpu_custom_call" | custom-call | tf_op jit(solution)/shard_map/exchange/pallas_call | solution.py:56
  446.9 0.0 copy-start.6
  446.9 20.7 %reshape.71 = f32[512,2,64,32]{3,2,1,0:T(8,128)} reshape(f32[128,8,16,128]{3,2,1,0:T(8,128)} %exchange.3) | data formatting | bytes 16777216 | tf_op jit(solution)/shard_map/reshape | solution.py:111
  467.7 0.0 copy-done.6
  467.7 0.0 copy-start.1
  467.7 98.7 %fusion = f32[2,64,32,512]{3,2,1,0:T(8,128)} fusion(f32[512,2,64,32]{3,2,1,0:T(8,128)} %reshape.71, f32[512,512]{1,0:T(8,128)S(1)} %copy-done.6), kind=kOutput, calls=%fused_computation.1 | convolution fusion | flops 6442450944 | bytes 17825792 | tf_op jit(solution)/shard_map/zk,kcxy->cxyz/dot_general | solution.py:112
  566.4 0.0 copy-done.1
  (3 shorter events, 0.0 us)
Async XLA Ops:
  0.0 1.2 copy-start
  218.3 14.3 %copy-start.3 = (f32[512,512]{1,0:T(8,128)S(1)}, f32[512,512]{1,0:T(8,128)}, u32[]{:S(2)}) copy-start(f32[512,512]{1,0:T(8,128)} %param.13) | copy-start | bytes 3145732
  232.6 9.9 %copy-start.4 = (f32[512,512]{1,0:T(8,128)S(1)}, f32[512,512]{1,0:T(8,128)}, u32[]{:S(2)}) copy-start(f32[512,512]{1,0:T(8,128)} %param.14) | copy-start | bytes 3145732
  242.4 15.8 %copy-start.10 = (s32[2]{0:T(128)S(1)}, s32[2]{0:T(128)}, u32[]{:S(2)}) copy-start(s32[2]{0:T(128)} %param.23) | copy-start | bytes 28
  242.4 15.8 %copy-start.2 = (f32[64]{0:T(128)S(1)}, f32[64]{0:T(128)}, u32[]{:S(2)}) copy-start(f32[64]{0:T(128)} %param.22) | copy-start | bytes 772
  242.4 17.2 %copy-start.8 = (f32[512]{0:T(512)S(1)}, f32[512]{0:T(512)}, u32[]{:S(2)}) copy-start(f32[512]{0:T(512)} %param.19) | copy-start | bytes 6148
  242.5 17.3 %copy-start.7 = (f32[512]{0:T(512)S(1)}, f32[512]{0:T(512)}, u32[]{:S(2)}) copy-start(f32[512]{0:T(512)} %param.20) | copy-start | bytes 6148
  242.5 17.6 %copy-start.9 = (f32[512,512]{1,0:T(8,128)S(1)}, f32[512,512]{1,0:T(8,128)}, u32[]{:S(2)}) copy-start(f32[512,512]{1,0:T(8,128)} %param.16) | copy-start | bytes 3145732
  260.1 12.2 %copy-start.5 = (f32[512,512]{1,0:T(8,128)S(1)}, f32[512,512]{1,0:T(8,128)}, u32[]{:S(2)}) copy-start(f32[512,512]{1,0:T(8,128)} %param.17) | copy-start | bytes 3145732
  446.9 20.8 %copy-start.6 = (f32[512,512]{1,0:T(8,128)S(1)}, f32[512,512]{1,0:T(8,128)}, u32[]{:S(2)}) copy-start(f32[512,512]{1,0:T(8,128)} %param.18) | copy-start | bytes 3145732
  467.7 98.7 %copy-start.1 = (f32[512,512]{1,0:T(8,128)S(1)}, f32[512,512]{1,0:T(8,128)}, u32[]{:S(2)}) copy-start(f32[512,512]{1,0:T(8,128)} %param.15) | copy-start | bytes 3145732

commit v2 on v1

v2 whole, which is shorter than its diff:
```python
import jax
import jax.numpy as jnp
from jax import lax
from jax.experimental import pallas as pl
from jax.experimental.pallas import tpu as pltpu
from jax.sharding import PartitionSpec as P

MESH = pl.DeviceIdType.MESH
F32, BF16 = jnp.float32, jnp.bfloat16
NT = (((1,), (1,)), ((), ()))
NN = (((1,), (0,)), ((), ()))
LANES = 128


def split(value):
    high = value.astype(BF16)
    return high, (value - high.astype(F32)).astype(BF16)


def product(left, right, dims):
    def dot(a, b):
        return lax.dot_general(a, b, dims, preferred_element_type=F32)

    return dot(left[0], right[0]) + dot(left[1], right[0]) + dot(left[0], right[1])


def solve_kernel(
    shift_index,
    shift_table,
    eig_z,
    eig_x,
    eig_y,
    columns,
    basis_in_x,
    basis_in_y,
    basis_in_z,
    basis_out_x,
    basis_out_y,
    basis_out_z,
    solved,
    cube,
    lines_high,
    lines_low,
    send_there,
    planes,
    send_back,
    returned,
    stacked,
    bases_high,
    bases_low,
    first_high,
    first_low,
    second_high,
    second_low,
    eig_sum,
    load_sem,
    store_sem,
    own_there_sem,
    own_back_sem,
    there_sem,
    back_sem,
    there_recv,
    back_recv,
):
    grp_count, pen_count = lax.axis_size("grp"), lax.axis_size("pen")
    count = grp_count * pen_count
    cols, cells, length = columns.shape
    slots = length // count
    steps = cols * slots
    rows = cells // LANES
    y_local = length // pen_count
    x_local = length // grp_count
    me = lax.axis_index("grp") * pen_count + lax.axis_index("pen")

    def place(t):
        return {"grp": t // pen_count, "pen": t % pen_count}

    bases = (basis_in_z, basis_in_y, basis_in_x, basis_out_x, basis_out_y, basis_out_z)
    lane_parts = length // LANES

    def base_part(b, part):
        return pltpu.make_async_copy(
            bases[b].at[:, pl.ds(part * LANES, LANES)],
            send_back.at[b, pl.ds(part * length, length), :],
            load_sem.at[cols + b],
        )

    def column_load(c, part):
        lanes = pl.ds(part * LANES, LANES)
        return pltpu.make_async_copy(columns.at[c, :, lanes], cube.at[c, part], load_sem.at[c])

    def column_wait(c):
        pltpu.make_async_copy(cube.at[c], cube.at[c], load_sem.at[c]).wait()

    for part in range(lane_parts):
        base_part(0, part).start()
    for c in range(cols):
        for part in range(lane_parts):
            column_load(c, part).start()
    for b in range(1, len(bases)):
        for part in range(lane_parts):
            base_part(b, part).start()

    barrier = pltpu.get_barrier_semaphore()

    def greet(i, carry):
        pl.semaphore_signal(
            barrier, inc=1, device_id=place((me + i) % count), device_id_type=MESH
        )
        return carry

    lax.fori_loop(1, count, greet, 0)

    def base_wait(b):
        whole = send_back.at[b]
        pltpu.make_async_copy(whole, whole, load_sem.at[cols + b]).wait()

    base_wait(0)
    for part in range(lane_parts):
        for slot in range(slots):
            start = part * length + slot * count
            high, low = split(send_back[0, start : start + count, :])
            lanes = slice(part * LANES, (part + 1) * LANES)
            stacked[2 * slot * count : (2 * slot + 1) * count, lanes] = high
            stacked[(2 * slot + 1) * count : (2 * slot + 2) * count, lanes] = low

    def prepare(c):
        def one(y, carry):
            to = pl.ds(
                pl.multiple_of((y % rows) * LANES + (y // rows) * x_local, x_local), x_local
            )
            for part in range(lane_parts):
                here = cube[c, part, pl.ds(y, x_local, stride=y_local), :]
                lanes = slice(part * LANES, (part + 1) * LANES)
                lines_high[to, lanes], lines_low[to, lanes] = split(here)
                cube[c, part, pl.ds(y, x_local, stride=y_local), :] = jnp.zeros_like(here)
            return carry

        lax.fori_loop(0, y_local, one, 0)

    def send_all(s, source, target, send_sem, recv_sem, own_sem):
        mine = pl.ds(pl.multiple_of(me * rows, rows), rows)
        pltpu.make_async_copy(source.at[s, mine, :], target.at[s, mine, :], own_sem.at[s]).start()

        def one(i, carry):
            t = (me + i) % count
            pltpu.make_async_remote_copy(
                src_ref=source.at[s, pl.ds(pl.multiple_of(t * rows, rows), rows), :],
                dst_ref=target.at[s, mine, :],
                send_sem=send_sem,
                recv_sem=recv_sem.at[s],
                device_id=place(t),
                device_id_type=MESH,
            ).start()
            return carry

        lax.fori_loop(1, count, one, 0)

    def receive_all(s, target, recv_sem, own_sem):
        own = target.at[s, pl.ds(0, rows), :]
        pltpu.make_async_copy(own, own, own_sem.at[s]).wait()
        others = target.at[s, pl.ds(0, (count - 1) * rows), :]
        pltpu.make_async_copy(others, others, recv_sem.at[s]).wait()

    def transform_lines(s):
        slot = s % slots
        both = stacked[pl.ds(pl.multiple_of(2 * slot * count, count), 2 * count), :]
        width = 4 * LANES

        def part(n, carry):
            where = pl.ds(pl.multiple_of(n * width, width), width)
            with_high = lax.dot_general(both, lines_high[where, :], NT, preferred_element_type=F32)
            with_low = lax.dot_general(
                both[:count], lines_low[where, :], NT, preferred_element_type=F32
            )
            value = with_high[:count] + with_high[count:] + with_low
            for q in range(4):
                send_there[s, pl.ds(n * 4 + q, count, stride=rows), :] = value[
                    :, q * LANES : (q + 1) * LANES
                ]
            return carry

        lax.fori_loop(0, cells // width, part, 0)

    for c in range(cols):
        column_wait(c)
        prepare(c)
        if c == 0:
            transform_lines(0)
            pl.semaphore_wait(barrier, count - 1)
            send_all(0, send_there, planes, there_sem, there_recv, own_there_sem)

        def forward(s, carry):
            transform_lines(s)
            send_all(s, send_there, planes, there_sem, there_recv, own_there_sem)
            return carry

        lax.fori_loop(1 if c == 0 else c * slots, (c + 1) * slots, forward, 0)

    for b in range(1, len(bases)):
        base_wait(b)
        for part in range(lane_parts):
            high, low = split(send_back[b, part * length : (part + 1) * length, :])
            lanes = slice(part * LANES, (part + 1) * LANES)
            bases_high[b - 1, :, lanes] = high
            bases_low[b - 1, :, lanes] = low
    eig_y_down = jnp.broadcast_to(eig_y[...], (LANES, length)).T
    for part in range(lane_parts):
        lanes = slice(part * LANES, (part + 1) * LANES)
        eig_sum[:, lanes] = eig_x[:, lanes] + eig_y_down

    first_half = lax.broadcasted_iota(jnp.int32, (1, LANES), 1) < x_local
    half = 2 * LANES

    def solve_plane(s):
        slot = s % slots
        shift = shift_table[shift_index[s // slots]]
        eig_z_here = eig_z[slot * count + me]
        block = pen_count * rows
        for h in range(lane_parts):
            a = planes[s, 2 * h * block : (2 * h + 1) * block, :]
            b = planes[s, (2 * h + 1) * block : (2 * h + 2) * block, :]
            low_y = jnp.where(first_half, a, pltpu.roll(b, x_local, 1))
            high_y = jnp.where(first_half, pltpu.roll(a, x_local, 1), b)
            low_y = low_y.reshape(pen_count, 1, rows, LANES)
            high_y = high_y.reshape(pen_count, 1, rows, LANES)
            both = jnp.concatenate([low_y, high_y], axis=1).reshape(length, LANES)
            lanes = slice(h * LANES, (h + 1) * LANES)
            first_high[:, lanes], first_low[:, lanes] = split(both)
        for n in range(length // half):
            lanes = slice(n * half, (n + 1) * half)
            value = product(
                (bases_high[0], bases_low[0]), (first_high[:, lanes], first_low[:, lanes]), NN
            )
            second_high[:, lanes], second_low[:, lanes] = split(value)
        scaling = jnp.sqrt(jnp.full((1, half), 2.0 * shift, F32))
        for n in range(length // half):
            lanes = slice(n * half, (n + 1) * half)
            value = product(
                (second_high[...], second_low[...]),
                (bases_high[1, lanes, :], bases_low[1, lanes, :]),
                NT,
            )
            value = scaling * value / (eig_sum[:, lanes] + eig_z_here + shift)
            first_high[:, lanes], first_low[:, lanes] = split(value)
        for n in range(length // half):
            lanes = slice(n * half, (n + 1) * half)
            value = product(
                (first_high[...], first_low[...]),
                (bases_high[2, lanes, :], bases_low[2, lanes, :]),
                NT,
            )
            second_high[:, lanes], second_low[:, lanes] = split(value)
        for n in range(length // half):
            lanes = slice(n * half, (n + 1) * half)
            value = product(
                (bases_high[3], bases_low[3]), (second_high[:, lanes], second_low[:, lanes]), NN
            )
            for i in range(2):
                h = 2 * n + i
                part = value[:, i * LANES : (i + 1) * LANES].reshape(pen_count, 2, rows, LANES)
                low_y = part[:, 0].reshape(block, LANES)
                high_y = part[:, 1].reshape(block, LANES)
                send_back[s, 2 * h * block : (2 * h + 1) * block, :] = jnp.where(
                    first_half, low_y, pltpu.roll(high_y, x_local, 1)
                )
                send_back[s, (2 * h + 1) * block : (2 * h + 2) * block, :] = jnp.where(
                    first_half, pltpu.roll(low_y, x_local, 1), high_y
                )

    def middle(s, carry):
        receive_all(s, planes, there_recv, own_there_sem)
        solve_plane(s)
        send_all(s, send_back, returned, back_sem, back_recv, own_back_sem)
        return carry

    lax.fori_loop(0, steps, middle, 0)

    def restore_lines(s):
        c, slot = s // slots, s % slots
        ks = pl.ds(pl.multiple_of(slot * count, count), count)
        right = (bases_high[4, :, ks], bases_low[4, :, ks])
        group = 4

        def part(n, carry):
            left = jnp.concatenate(
                [
                    returned[s, pl.ds(n * group + q, count, stride=rows), :].T
                    for q in range(group)
                ],
                axis=0,
            )
            value = product(split(left), right, NT)
            for q in range(group):
                for high in range(LANES // x_local):
                    start = q * LANES + high * x_local
                    y = high * rows + n * group + q
                    to = pl.ds(y, x_local, stride=y_local)
                    for p in range(lane_parts):
                        cube[c, p, to, :] = (
                            cube[c, p, to, :]
                            + value[start : start + x_local, p * LANES : (p + 1) * LANES]
                        )
            return carry

        lax.fori_loop(0, rows // group, part, 0)

    def backward(s, carry):
        receive_all(s, returned, back_recv, own_back_sem)
        restore_lines(s)
        return carry

    def column_store(c, part):
        lanes = pl.ds(part * LANES, LANES)
        return pltpu.make_async_copy(cube.at[c, part], solved.at[c, :, lanes], store_sem.at[c])

    for c in range(cols):
        lax.fori_loop(c * slots, (c + 1) * slots, backward, 0)
        for part in range(lane_parts):
            column_store(c, part).start()
    sent = pl.ds(0, (count - 1) * rows)
    for source, sem in ((send_there, there_sem), (send_back, back_sem)):
        whole = source.at[:, sent, :]
        pltpu.make_async_copy(whole, whole, sem).wait()
    for c in range(cols):
        pltpu.make_async_copy(cube.at[c], cube.at[c], store_sem.at[c]).wait()


def per_device(
    columns,
    basis_in_x,
    basis_in_y,
    basis_in_z,
    basis_out_x,
    basis_out_y,
    basis_out_z,
    eig_x,
    eig_y,
    eig_z,
    shift_table,
    shift_index,
):
    cols, x_local, y_local, length = columns.shape
    cells = x_local * y_local
    count = lax.axis_size("grp") * lax.axis_size("pen")
    slots = length // count
    steps = cols * slots
    smem = pl.BlockSpec(memory_space=pltpu.SMEM)
    vmem = pl.BlockSpec(memory_space=pltpu.VMEM)
    far = pl.BlockSpec(memory_space=pl.ANY)
    messages = pltpu.VMEM((steps, cells * count // LANES, LANES), F32)
    square = pltpu.VMEM((length, length), BF16)
    dma = pltpu.SemaphoreType.DMA
    solved = pl.pallas_call(
        solve_kernel,
        out_shape=jax.ShapeDtypeStruct((cols, cells, length), F32),
        in_specs=[smem, smem, smem, vmem, vmem] + [far] * 7,
        out_specs=far,
        scratch_shapes=[
            pltpu.VMEM((cols, length // LANES, cells, LANES), F32),
            pltpu.VMEM((cells, length), BF16),
            pltpu.VMEM((cells, length), BF16),
            messages,
            messages,
            messages,
            messages,
            pltpu.VMEM((2 * length, length), BF16),
            pltpu.VMEM((5, length, length), BF16),
            pltpu.VMEM((5, length, length), BF16),
            square,
            square,
            square,
            square,
            pltpu.VMEM((length, length), F32),
            dma((cols + 6,)),
            dma((cols,)),
            dma((steps,)),
            dma((steps,)),
            dma,
            dma,
            dma((steps,)),
            dma((steps,)),
        ],
        compiler_params=pltpu.CompilerParams(
            collective_id=0, has_side_effects=True, vmem_limit_bytes=67043328
        ),
        name="solve",
    )(
        shift_index,
        shift_table,
        eig_z,
        eig_x.reshape(1, length),
        eig_y.reshape(1, length),
        columns.reshape(cols, cells, length),
        basis_in_x,
        basis_in_y,
        basis_in_z,
        basis_out_x,
        basis_out_y,
        basis_out_z,
    )
    return solved.reshape(columns.shape)


def solution(mesh):
    in_specs = (P(None, "grp", "pen", None), P(), P(), P(), P(), P(), P(), P(), P(), P(), P(), P())
    out_specs = P(None, "grp", "pen", None)
    return jax.shard_map(
        per_device, mesh=mesh, in_specs=in_specs, out_specs=out_specs, check_vma=False
    )
```

time: 577 us -> 306 us (0.53)
  the two profiles are of different devices: /device:TPU:33 before, /device:TPU:61 now
where the time goes in v2:
time: 306 us; the launch traced here: 305 us
  Pallas kernels  297 us (97%)
  local copies, waits for them, and re-layouts  8.65 us (3%)
    pallas_call x1, Pallas kernels, per_device(): pl.pallas_call(solve_kernel, out_shape=jax.ShapeDtypeStruct((cols, cells,...  297 us
    unnamed x1, local copies, waits for them, and re-layouts  8.65 us

profile of v2, /device:TPU:61, one launch (start us, length us, event | category | flops | bytes accessed | tf_op | source)
XLA Modules:
  0.0 305.4 jit_solution(4997232432210707407)
XLA Ops:
  0.0 296.7 %solve.1 = f32[2,2048,512]{2,1,0:T(8,128)} custom-call(s32[2]{0:T(128)} %shift_index.1, f32[64]{0:T(128)} %shift_table.1, f32[512]{0:T(512)} %eig_z.1, f32[1,512]{1,0:T(1,128)} %bitcast.6, f32[1,512]{1,0:T(1,128)} %bitcast.7, f32[2,2048,512]{2,1,0:T(8,128)} %bitcast.5, f32[512,512]{1,0:T(8,128)} %basis_in_x.1, f32[512,512]{1,0:T(8,128)} %basis_in_y.1, ...), custom_call_target="tpu_custom_call" | custom-call | tf_op jit(solution)/shard_map/solve/pallas_call | solution.py:354
  296.7 8.6 %copy.14 = f32[2,64,32,512]{3,2,1,0:T(8,128)} copy(f32[2,64,32,512]{3,2,1,0:T(8,128)} %bitcast.4) | data formatting | bytes 16777216

commit v3 on v2

--- a/solution.py
+++ b/solution.py
@@ -75,7 +75,17 @@
     def place(t):
         return {"grp": t // pen_count, "pen": t % pen_count}
 
-    bases = (basis_in_z, basis_in_y, basis_in_x, basis_out_x, basis_out_y, basis_out_z)
+    chip_x, chip_y = me // 2 % 4, me // pen_count % 4
+    chip_z, core = me // 8 % 2 * 2 + me // 64, me % 2
+
+    def flat(dx, dy, dz, dc):
+        z = (chip_z + dz) % 4
+        return (
+            (z % 2) * 64 + (chip_y + dy) % 4 * 16 + (z // 2) * 8 + (chip_x + dx) % 4 * 2
+            + (core + dc) % 2
+        )
+
+    bases = (basis_in_z, basis_in_x, basis_in_y, basis_out_y, basis_out_x, basis_out_z)
     lane_parts = length // LANES
 
     def base_part(b, part):
@@ -85,18 +95,13 @@
             load_sem.at[cols + b],
         )
 
-    def column_load(c, part):
-        lanes = pl.ds(part * LANES, LANES)
-        return pltpu.make_async_copy(columns.at[c, :, lanes], cube.at[c, part], load_sem.at[c])
-
-    def column_wait(c):
-        pltpu.make_async_copy(cube.at[c], cube.at[c], load_sem.at[c]).wait()
+    def column_load(c):
+        return pltpu.make_async_copy(columns.at[c], cube.at[c], load_sem.at[c])
 
     for part in range(lane_parts):
         base_part(0, part).start()
     for c in range(cols):
-        for part in range(lane_parts):
-            column_load(c, part).start()
+        column_load(c).start()
     for b in range(1, len(bases)):
         for part in range(lane_parts):
             base_part(b, part).start()
@@ -124,37 +129,43 @@
             stacked[2 * slot * count : (2 * slot + 1) * count, lanes] = high
             stacked[(2 * slot + 1) * count : (2 * slot + 2) * count, lanes] = low
 
+    def cell_block(group, r):
+        return pl.ds(pl.multiple_of((r * rows + group) * y_local, y_local), y_local)
+
     def prepare(c):
-        def one(y, carry):
-            to = pl.ds(
-                pl.multiple_of((y % rows) * LANES + (y // rows) * x_local, x_local), x_local
-            )
-            for part in range(lane_parts):
-                here = cube[c, part, pl.ds(y, x_local, stride=y_local), :]
-                lanes = slice(part * LANES, (part + 1) * LANES)
-                lines_high[to, lanes], lines_low[to, lanes] = split(here)
-                cube[c, part, pl.ds(y, x_local, stride=y_local), :] = jnp.zeros_like(here)
+        def one(x, carry):
+            group, r = x % rows, x // rows
+            to = pl.ds(pl.multiple_of(group * LANES + r * y_local, y_local), y_local)
+            lines_high[to, :], lines_low[to, :] = split(cube[c, cell_block(group, r), :])
             return carry
 
-        lax.fori_loop(0, y_local, one, 0)
+        lax.fori_loop(0, x_local, one, 0)
 
     def send_all(s, source, target, send_sem, recv_sem, own_sem):
         mine = pl.ds(pl.multiple_of(me * rows, rows), rows)
         pltpu.make_async_copy(source.at[s, mine, :], target.at[s, mine, :], own_sem.at[s]).start()
 
-        def one(i, carry):
-            t = (me + i) % count
-            pltpu.make_async_remote_copy(
-                src_ref=source.at[s, pl.ds(pl.multiple_of(t * rows, rows), rows), :],
-                dst_ref=target.at[s, mine, :],
-                send_sem=send_sem,
-                recv_sem=recv_sem.at[s],
-                device_id=place(t),
-                device_id_type=MESH,
-            ).start()
+        def some(i, carry):
+            for u in range(4):
+                for v in range(4):
+
+                    def one(t=flat(u, u + v, u + i % 4, i // 4)):
+                        pltpu.make_async_remote_copy(
+                            src_ref=source.at[s, pl.ds(pl.multiple_of(t * rows, rows), rows), :],
+                            dst_ref=target.at[s, mine, :],
+                            send_sem=send_sem,
+                            recv_sem=recv_sem.at[s],
+                            device_id=place(t),
+                            device_id_type=MESH,
+                        ).start()
+
+                    if u == 0 and v == 0:
+                        pl.when(i > 0)(one)
+                    else:
+                        one()
             return carry
 
-        lax.fori_loop(1, count, one, 0)
+        lax.fori_loop(0, 8, some, 0)
 
     def receive_all(s, target, recv_sem, own_sem):
         own = target.at[s, pl.ds(0, rows), :]
@@ -183,7 +194,7 @@
         lax.fori_loop(0, cells // width, part, 0)
 
     for c in range(cols):
-        column_wait(c)
+        column_load(c).wait()
         prepare(c)
         if c == 0:
             transform_lines(0)
@@ -204,29 +215,49 @@
             lanes = slice(part * LANES, (part + 1) * LANES)
             bases_high[b - 1, :, lanes] = high
             bases_low[b - 1, :, lanes] = low
-    eig_y_down = jnp.broadcast_to(eig_y[...], (LANES, length)).T
+    eig_x_down = jnp.broadcast_to(eig_x[...], (LANES, length)).T
     for part in range(lane_parts):
         lanes = slice(part * LANES, (part + 1) * LANES)
-        eig_sum[:, lanes] = eig_x[:, lanes] + eig_y_down
-
-    first_half = lax.broadcasted_iota(jnp.int32, (1, LANES), 1) < x_local
+        eig_sum[:, lanes] = eig_x_down + eig_y[:, lanes]
+
+    lane = lax.broadcasted_iota(jnp.int32, (1, LANES), 1)
+    first_half = lane < 2 * y_local
+    even_part = lane % (2 * y_local) < y_local
+
+    def exchange_parts(parts):
+        def swap(a, b, keep, shift):
+            return (
+                jnp.where(keep, a, pltpu.roll(b, shift, 1)),
+                jnp.where(keep, pltpu.roll(a, LANES - shift, 1), b),
+            )
+
+        a0, a1, a2, a3 = (parts[rows * j : rows * (j + 1)] for j in range(4))
+        b0, b2 = swap(a0, a2, first_half, 2 * y_local)
+        b1, b3 = swap(a1, a3, first_half, 2 * y_local)
+        return jnp.concatenate(
+            [*swap(b0, b1, even_part, y_local), *swap(b2, b3, even_part, y_local)], axis=0
+        )
+
+    def clear(i, carry):
+        here = pl.ds(pl.multiple_of(i * y_local, y_local), y_local)
+        for c in range(cols):
+            cube[c, here, :] = jnp.zeros((y_local, length), F32)
+        return carry
+
+    lax.fori_loop(0, x_local, clear, 0)
+
     half = 2 * LANES
 
     def solve_plane(s):
         slot = s % slots
         shift = shift_table[shift_index[s // slots]]
         eig_z_here = eig_z[slot * count + me]
-        block = pen_count * rows
-        for h in range(lane_parts):
-            a = planes[s, 2 * h * block : (2 * h + 1) * block, :]
-            b = planes[s, (2 * h + 1) * block : (2 * h + 2) * block, :]
-            low_y = jnp.where(first_half, a, pltpu.roll(b, x_local, 1))
-            high_y = jnp.where(first_half, pltpu.roll(a, x_local, 1), b)
-            low_y = low_y.reshape(pen_count, 1, rows, LANES)
-            high_y = high_y.reshape(pen_count, 1, rows, LANES)
-            both = jnp.concatenate([low_y, high_y], axis=1).reshape(length, LANES)
-            lanes = slice(h * LANES, (h + 1) * LANES)
-            first_high[:, lanes], first_low[:, lanes] = split(both)
+        for g in range(grp_count):
+            for q in range(lane_parts):
+                start = (g * pen_count + 4 * q) * rows
+                block = exchange_parts(planes[s, start : start + 4 * rows, :])
+                here, lanes = slice(g * x_local, (g + 1) * x_local), slice(q * LANES, (q + 1) * LANES)
+                first_high[here, lanes], first_low[here, lanes] = split(block)
         for n in range(length // half):
             lanes = slice(n * half, (n + 1) * half)
             value = product(
@@ -257,16 +288,11 @@
                 (bases_high[3], bases_low[3]), (second_high[:, lanes], second_low[:, lanes]), NN
             )
             for i in range(2):
-                h = 2 * n + i
-                part = value[:, i * LANES : (i + 1) * LANES].reshape(pen_count, 2, rows, LANES)
-                low_y = part[:, 0].reshape(block, LANES)
-                high_y = part[:, 1].reshape(block, LANES)
-                send_back[s, 2 * h * block : (2 * h + 1) * block, :] = jnp.where(
-                    first_half, low_y, pltpu.roll(high_y, x_local, 1)
-                )
-                send_back[s, (2 * h + 1) * block : (2 * h + 2) * block, :] = jnp.where(
-                    first_half, pltpu.roll(low_y, x_local, 1), high_y
-                )
+                for g in range(grp_count):
+                    start = (g * pen_count + 4 * (2 * n + i)) * rows
+                    send_back[s, start : start + 4 * rows, :] = exchange_parts(
+                        value[g * x_local : (g + 1) * x_local, i * LANES : (i + 1) * LANES]
+                    )
 
     def middle(s, carry):
         receive_all(s, planes, there_recv, own_there_sem)
@@ -292,15 +318,10 @@
             )
             value = product(split(left), right, NT)
             for q in range(group):
-                for high in range(LANES // x_local):
-                    start = q * LANES + high * x_local
-                    y = high * rows + n * group + q
-                    to = pl.ds(y, x_local, stride=y_local)
-                    for p in range(lane_parts):
-                        cube[c, p, to, :] = (
-                            cube[c, p, to, :]
-                            + value[start : start + x_local, p * LANES : (p + 1) * LANES]
-                        )
+                for r in range(LANES // y_local):
+                    start = q * LANES + r * y_local
+                    here = cell_block(n * group + q, r)
+                    cube[c, here, :] = cube[c, here, :] + value[start : start + y_local]
             return carry
 
         lax.fori_loop(0, rows // group, part, 0)
@@ -310,20 +331,18 @@
         restore_lines(s)
         return carry
 
-    def column_store(c, part):
-        lanes = pl.ds(part * LANES, LANES)
-        return pltpu.make_async_copy(cube.at[c, part], solved.at[c, :, lanes], store_sem.at[c])
+    def column_store(c):
+        return pltpu.make_async_copy(cube.at[c], solved.at[c], store_sem.at[c])
 
     for c in range(cols):
         lax.fori_loop(c * slots, (c + 1) * slots, backward, 0)
-        for part in range(lane_parts):
-            column_store(c, part).start()
+        column_store(c).start()
     sent = pl.ds(0, (count - 1) * rows)
     for source, sem in ((send_there, there_sem), (send_back, back_sem)):
         whole = source.at[:, sent, :]
         pltpu.make_async_copy(whole, whole, sem).wait()
     for c in range(cols):
-        pltpu.make_async_copy(cube.at[c], cube.at[c], store_sem.at[c]).wait()
+        column_store(c).wait()
 
 
 def per_device(
@@ -357,7 +376,7 @@
         in_specs=[smem, smem, smem, vmem, vmem] + [far] * 7,
         out_specs=far,
         scratch_shapes=[
-            pltpu.VMEM((cols, length // LANES, cells, LANES), F32),
+            pltpu.VMEM((cols, cells, length), F32),
             pltpu.VMEM((cells, length), BF16),
             pltpu.VMEM((cells, length), BF16),
             messages,

time: 306 us -> 211 us (0.69)
  the two profiles are of different devices: /device:TPU:61 before, /device:TPU:1 now
where the time goes in v3:
time: 211 us
  Pallas kernels  203 us (96%)
  local copies, waits for them, and re-layouts  8.65 us (4%)
    pallas_call x1, Pallas kernels, per_device(): pl.pallas_call(solve_kernel, out_shape=jax.ShapeDtypeStruct((cols, cells,...  203 us
    unnamed x1, local copies, waits for them, and re-layouts  8.65 us

profile of v3, /device:TPU:1, one launch (start us, length us, event | category | flops | bytes accessed | tf_op | source)
XLA Modules:
  0.0 211.2 jit_solution(17771918514471009299)
XLA Ops:
  0.0 202.5 %solve.1 = f32[2,2048,512]{2,1,0:T(8,128)} custom-call(s32[2]{0:T(128)} %shift_index.1, f32[64]{0:T(128)} %shift_table.1, f32[512]{0:T(512)} %eig_z.1, f32[1,512]{1,0:T(1,128)} %bitcast.6, f32[1,512]{1,0:T(1,128)} %bitcast.7, f32[2,2048,512]{2,1,0:T(8,128)} %bitcast.5, f32[512,512]{1,0:T(8,128)} %basis_in_x.1, f32[512,512]{1,0:T(8,128)} %basis_in_y.1, ...), custom_call_target="tpu_custom_call" | custom-call | tf_op jit(solution)/shard_map/solve/pallas_call | solution.py:373
  202.6 8.6 %copy.14 = f32[2,64,32,512]{3,2,1,0:T(8,128)} copy(f32[2,64,32,512]{3,2,1,0:T(8,128)} %bitcast.4) | data formatting | bytes 16777216

commit v4 on v3

--- a/solution.py
+++ b/solution.py
@@ -37,7 +37,6 @@
     basis_out_x,
     basis_out_y,
     basis_out_z,
-    solved,
     cube,
     lines_high,
     lines_low,
@@ -54,7 +53,6 @@
     second_low,
     eig_sum,
     load_sem,
-    store_sem,
     own_there_sem,
     own_back_sem,
     there_sem,
@@ -331,18 +329,12 @@
         restore_lines(s)
         return carry
 
-    def column_store(c):
-        return pltpu.make_async_copy(cube.at[c], solved.at[c], store_sem.at[c])
-
     for c in range(cols):
         lax.fori_loop(c * slots, (c + 1) * slots, backward, 0)
-        column_store(c).start()
     sent = pl.ds(0, (count - 1) * rows)
     for source, sem in ((send_there, there_sem), (send_back, back_sem)):
         whole = source.at[:, sent, :]
         pltpu.make_async_copy(whole, whole, sem).wait()
-    for c in range(cols):
-        column_store(c).wait()
 
 
 def per_device(
@@ -372,11 +364,10 @@
     dma = pltpu.SemaphoreType.DMA
     solved = pl.pallas_call(
         solve_kernel,
-        out_shape=jax.ShapeDtypeStruct((cols, cells, length), F32),
+        out_shape=pltpu.VMEM((cols, cells, length), F32),
         in_specs=[smem, smem, smem, vmem, vmem] + [far] * 7,
-        out_specs=far,
+        out_specs=vmem,
         scratch_shapes=[
-            pltpu.VMEM((cols, cells, length), F32),
             pltpu.VMEM((cells, length), BF16),
             pltpu.VMEM((cells, length), BF16),
             messages,
@@ -392,7 +383,6 @@
             square,
             pltpu.VMEM((length, length), F32),
             dma((cols + 6,)),
-            dma((cols,)),
             dma((steps,)),
             dma((steps,)),
             dma,
@@ -401,7 +391,7 @@
             dma((steps,)),
         ],
         compiler_params=pltpu.CompilerParams(
-            collective_id=0, has_side_effects=True, vmem_limit_bytes=67043328
+            collective_id=0, has_side_effects=True, vmem_limit_bytes=54 * 2**20
         ),
         name="solve",
     )(

time: 211 us -> 204 us (0.967)
  local copies, waits for them, and re-layouts: 8.65 us -> 3.4 us
    unnamed x1, local copies, waits for them, and re-layouts: 8.65 us -> 3.4 us
where the time goes in v4:
time: 204 us
  Pallas kernels  201 us (99%)
  local copies, waits for them, and re-layouts  3.4 us (2%)
    pallas_call x1, Pallas kernels, per_device(): pl.pallas_call(solve_kernel, out_shape=pltpu.VMEM((cols, cells, length),...  201 us

profile of v4, /device:TPU:1, one launch (start us, length us, event | category | flops | bytes accessed | tf_op | source)
XLA Modules:
  0.0 204.0 jit_solution(17897555694998151014)
XLA Ops:
  0.0 200.6 %solve.1 = f32[2,2048,512]{2,1,0:T(8,128)S(1)} custom-call(s32[2]{0:T(128)} %shift_index.1, f32[64]{0:T(128)} %shift_table.1, f32[512]{0:T(512)} %eig_z.1, f32[1,512]{1,0:T(1,128)} %bitcast.6, f32[1,512]{1,0:T(1,128)} %bitcast.7, f32[2,2048,512]{2,1,0:T(8,128)} %bitcast.5, f32[512,512]{1,0:T(8,128)} %basis_in_x.1, f32[512,512]{1,0:T(8,128)} %basis_in_y.1, ...), custom_call_target="tpu_custom_call" | custom-call | tf_op jit(solution)/shard_map/solve/pallas_call | solution.py:365
  200.6 3.4 %copy.14 = f32[2,64,32,512]{3,2,1,0:T(8,128)} copy(f32[2,64,32,512]{3,2,1,0:T(8,128)S(1)} %bitcast.4) | data formatting | bytes 16777216

commit v5 on v4

--- a/solution.py
+++ b/solution.py
@@ -75,11 +75,12 @@
 
     chip_x, chip_y = me // 2 % 4, me // pen_count % 4
     chip_z, core = me // 8 % 2 * 2 + me // 64, me % 2
+    sign = 1 - 2 * core
 
     def flat(dx, dy, dz, dc):
-        z = (chip_z + dz) % 4
+        z = (chip_z + 8 + sign * dz) % 4
         return (
-            (z % 2) * 64 + (chip_y + dy) % 4 * 16 + (z // 2) * 8 + (chip_x + dx) % 4 * 2
+            (z % 2) * 64 + (chip_y + 8 + sign * dy) % 4 * 16 + (z // 2) * 8 + (chip_x + 8 + sign * dx) % 4 * 2
             + (core + dc) % 2
         )
 

time: 204 us -> 204 us (level)
  no operation moved by 1% of the time
where the time goes in v5:
time: 204 us
  Pallas kernels  201 us (99%)
  local copies, waits for them, and re-layouts  3.4 us (2%)
    pallas_call x1, Pallas kernels, per_device(): pl.pallas_call(solve_kernel, out_shape=pltpu.VMEM((cols, cells, length),...  201 us

profile of v5, /device:TPU:1, one launch (start us, length us, event | category | flops | bytes accessed | tf_op | source)
XLA Modules:
  0.0 204.1 jit_solution(16496048631121590753)
XLA Ops:
  0.0 200.6 %solve.1 = f32[2,2048,512]{2,1,0:T(8,128)S(1)} custom-call(s32[2]{0:T(128)} %shift_index.1, f32[64]{0:T(128)} %shift_table.1, f32[512]{0:T(512)} %eig_z.1, f32[1,512]{1,0:T(1,128)} %bitcast.6, f32[1,512]{1,0:T(1,128)} %bitcast.7, f32[2,2048,512]{2,1,0:T(8,128)} %bitcast.5, f32[512,512]{1,0:T(8,128)} %basis_in_x.1, f32[512,512]{1,0:T(8,128)} %basis_in_y.1, ...), custom_call_target="tpu_custom_call" | custom-call | tf_op jit(solution)/shard_map/solve/pallas_call | solution.py:366
  200.7 3.4 %copy.14 = f32[2,64,32,512]{3,2,1,0:T(8,128)} copy(f32[2,64,32,512]{3,2,1,0:T(8,128)S(1)} %bitcast.4) | data formatting | bytes 16777216
